TPU v7x, 256 devices: a whole 4x4x8 slice. The times are simulated.
256 devices in a mesh: patch: 32 (over y, z), req: 4 (over x), owner: 2 (over core).
Axes of the slice: x: 4, y: 4, z: 8, core: 2. Of those that a mesh axis runs over, the one named last changes fastest.
Arguments:
- latents: bfloat16 [8, 256, 256, 320], P('req', 'patch', 'owner'), may hold values from -24 to 24
- timestep_embedding: bfloat16 [8, 1280], P('req'), may hold values from -6 to 6
- embedding_weight: bfloat16 [1280, 320], replicated, may hold values from -0.15625 to 0.15625
- group_norm_gain: float32 [2, 320], replicated, may hold values from 0.25 to 1.75
- group_norm_shift: float32 [2, 320], replicated, may hold values from -3 to 3
- kernel_weight: bfloat16 [2, 9, 320, 320], replicated, may hold values from -0.109375 to 0.109375
- plugin_reduce_library: bfloat16 [8, 2, 184320], P(('req', 'owner'), None, 'patch'), may hold values from -0.109375 to 0.109375
- plugin_expand_library: bfloat16 [8, 2, 20480], P(('req', 'owner'), None, 'patch'), may hold values from -0.75 to 0.75
- image_adapter: int32 [8, 1], P('req'), may hold values from 0 to 7
- adapter_bank_row: int32 [8], replicated, may hold values from 0 to 7, each once
Outputs:
- result: bfloat16 [8, 256, 256, 320], P('req', 'patch', 'owner')
Inputs may be any that keep to these rules, and one draw needn't show every extreme that they name: `image_adapter`: each image names one adapter; every adapter is named by some image. A permutation: adapter a is stored in bank row adapter_bank_row[a].
All inputs are finite; a program needn't handle non-finite values.
Results may differ from a plain program's by a relative error of at most 0.0055.
Values may be sent and summed in bfloat16 or wider, within the bound.
A program may use at most 128 MiB of HBM per device.

v0:
```python
import jax
import jax.numpy as jnp
from jax import lax
from jax.sharding import PartitionSpec as P

GROUPS = 32


def padded_2(block, sides, width):
    for axis, dim in sides:
        count = lax.axis_size(axis)
        forward = [(i, i + 1) for i in range(count - 1)]
        backward = [(target, source) for source, target in forward]
        low = lax.ppermute(
            lax.slice_in_dim(block, block.shape[dim] - width, None, axis=dim), axis, forward
        )
        high = lax.ppermute(lax.slice_in_dim(block, 0, width, axis=dim), axis, backward)
        block = jnp.concatenate([low, block, high], axis=dim)
    return block


def group_act(values, gain, shift):
    images, rows, columns, chans = values.shape
    grouped = values.reshape(images, rows, columns, GROUPS, chans // GROUPS)
    count = rows * columns * (chans // GROUPS) * lax.axis_size("patch") * lax.axis_size("owner")
    total = lax.psum(jnp.sum(grouped, axis=(1, 2, 4)), ("patch", "owner"))
    mean = total / count
    centered = grouped - mean[:, None, None, :, None]
    spread = lax.psum(jnp.sum(centered * centered, axis=(1, 2, 4)), ("patch", "owner"))
    var = spread / count
    normed = (centered / jnp.sqrt(var + 1e-05)[:, None, None, :, None]).reshape(values.shape)
    return jax.nn.silu(normed * gain + shift).astype(jnp.bfloat16)


def block_conv(act, kernel, reducing_filter, expanding_linear_map):
    images, rows, columns, chans = act.shape
    outward = kernel.shape[2]
    padded = padded_2(act, (("patch", 1), ("owner", 2)), 1)
    joined = jnp.concatenate(
        [jnp.broadcast_to(kernel[None], (images,) + kernel.shape), reducing_filter], axis=3
    )
    accum = jnp.zeros((images, rows, columns, joined.shape[3]), jnp.float32)
    for tap in range(9):
        row_off, col_off = divmod(tap, 3)
        window = padded[:, row_off : row_off + rows, col_off : col_off + columns, :]
        accum = accum + jnp.einsum(
            "bhwc,bcd->bhwd", window, joined[:, tap], preferred_element_type=jnp.float32
        )
    lowpart = accum[..., outward:].astype(jnp.bfloat16)
    return accum[..., :outward] + jnp.einsum(
        "bhwr,brd->bhwd", lowpart, expanding_linear_map, preferred_element_type=jnp.float32
    )


def local(
    latents,
    timestep_embedding,
    embedding_weight,
    group_norm_gain,
    group_norm_shift,
    kernel_weight,
    plugin_reduce_library,
    plugin_expand_library,
    image_adapter,
    adapter_bank_row,
):
    images, rows, columns, chans = latents.shape
    wanted = image_adapter[:, 0]
    table = jnp.arange(adapter_bank_row.shape[0], dtype=jnp.int32)
    slots = jnp.sum(
        jnp.where(wanted[:, None] == table[None, :], adapter_bank_row[None, :], 0), axis=1
    )
    full_down, full_up = (
        lax.all_gather(plugin_reduce_library, "patch", axis=2, tiled=True),
        lax.all_gather(plugin_expand_library, "patch", axis=2, tiled=True),
    )
    pieces = (
        lax.all_gather(full_down, ("req", "owner"), axis=0, tiled=True),
        lax.all_gather(full_up, ("req", "owner"), axis=0, tiled=True),
    )
    count = pieces[0].shape[0]
    match = (slots[:, None] == jnp.arange(count, dtype=jnp.int32)[None, :]).astype(jnp.bfloat16)
    first = jnp.einsum("ik,kjs->ijs", match, pieces[0], preferred_element_type=jnp.float32)
    second = jnp.einsum("ik,kjs->ijs", match, pieces[1], preferred_element_type=jnp.float32)
    down_sel = first.astype(jnp.bfloat16)
    up_sel = second.astype(jnp.bfloat16)
    rank = up_sel.shape[2] // chans
    down_all = down_sel.reshape(images, 2, 9, chans, rank)
    up_all = up_sel.reshape(images, 2, rank, chans)
    temb = jax.nn.silu(timestep_embedding.astype(jnp.float32)).astype(jnp.bfloat16)
    proj = jnp.dot(temb, embedding_weight, preferred_element_type=jnp.float32)
    source = latents.astype(jnp.float32)
    act1 = group_act(source, group_norm_gain[0], group_norm_shift[0])
    hidden1 = (
        block_conv(act1, kernel_weight[0], down_all[:, 0], up_all[:, 0]) + proj[:, None, None, :]
    ).astype(jnp.bfloat16)
    act2 = group_act(hidden1.astype(jnp.float32), group_norm_gain[1], group_norm_shift[1])
    result = source + block_conv(act2, kernel_weight[1], down_all[:, 1], up_all[:, 1])
    return result.astype(jnp.bfloat16)


def solution(mesh):
    in_specs = (
        P("req", "patch", "owner", None),
        P("req", None),
        P(),
        P(),
        P(),
        P(),
        P(("req", "owner"), None, "patch"),
        P(("req", "owner"), None, "patch"),
        P("req", None),
        P(),
    )
    out_specs = P("req", "patch", "owner", None)
    return jax.shard_map(local, mesh=mesh, in_specs=in_specs, out_specs=out_specs, check_vma=False)
```

profile of v0, /device:TPU:1, one launch (start us, length us, event | category | flops | bytes accessed | tf_op | source)
XLA Modules:
  0.0 778.4 jit_solution(10491722644223189108)
XLA Ops:
  6.6 47.2 %all_gather.12 = bf16[1,2,184320]{2,1,0:T(2,128)(2,1)} all-gather(bf16[1,2,5760]{2,1,0:T(2,128)(2,1)} %param.16), channel_id=1, replica_groups=mesh['patch'=32,'req'=4,'owner'=2] {'patch'}, dimensions={2}, use_global_device_ids=true | all-gather | bytes 760320 | tf_op jit(solution)/shard_map/all_gather | solution.py:74
  53.9 1.6 convert_reduce_fusion
  55.6 135.6 %psum.28 = f32[2,32]{1,0:T(2,128)S(1)} all-reduce(f32[2,32]{1,0:T(2,128)S(1)} %reduce_sum.59), channel_id=1, replica_groups=mesh['patch'=32,'req'=4,'owner'=2] {'patch','owner'}, use_global_device_ids=true, to_apply=%region_2.3 | all-reduce | flops 64 | bytes 512 | tf_op jit(solution)/shard_map/psum | solution.py:26
  192.2 124.0 %psum.29 = f32[2,32]{1,0:T(2,128)S(1)} all-reduce(f32[2,32]{1,0:T(2,128)S(1)} %reduce_sum.62), channel_id=1, replica_groups=mesh['patch'=32,'req'=4,'owner'=2] {'patch','owner'}, use_global_device_ids=true, to_apply=%region_5.6 | all-reduce | flops 64 | bytes 512 | tf_op jit(solution)/shard_map/psum | solution.py:29
  316.5 1.4 multiply_convert_fusion.1
  320.5 32.0 %all_gather.14 = bf16[1,2,20480]{2,1,0:T(2,128)(2,1)S(1)} all-gather(bf16[1,2,640]{2,1,0:T(2,128)(2,1)S(1)} %copy-done.16), channel_id=1, replica_groups=mesh['patch'=32,'req'=4,'owner'=2] {'patch'}, dimensions={2}, use_global_device_ids=true | all-gather | bytes 84480 | tf_op jit(solution)/shard_map/all_gather | solution.py:75
  352.5 24.4 %all_gather.15 = bf16[8,2,20480]{2,1,0:T(2,128)(2,1)S(1)} all-gather(bf16[1,2,20480]{2,1,0:T(2,128)(2,1)S(1)} %all_gather.14), channel_id=1, replica_groups=mesh['patch'=32,'req'=4,'owner'=2] {'req','owner'}, dimensions={0}, use_global_device_ids=true | all-gather | bytes 737280 | tf_op jit(solution)/shard_map/all_gather | solution.py:79
  377.0 4.8 slice_bitcast_fusion
  382.5 2.5 fusion.147
  385.0 1.9 copy.87
  388.2 1.9 copy.94
  390.1 3.5 collective-permute-start.3
  394.7 1.7 copy.88
  396.3 1.6 copy.95
  398.0 5.7 pad_maximum_fusion
  403.7 10.7 %convolution_convert_fusion = bf16[2,2,184320]{2,0,1:T(2,128)(2,1)} fusion(bf16[8,2,184320]{2,1,0:T(2,128)(2,1)} %all-gather.2.cloned.1.call-done, s32[2]{0:T(128)S(1)} %fusion.123), kind=kOutput, calls=%fused_computation | convolution fusion | flops 12533776 | bytes 7372808 | tf_op jit(solution)/shard_map/ik,kjs->ijs/dot_general | solution.py:83
  414.4 4.7 reshape.54
  419.1 3.3 fusion.145
  425.4 2.7 fusion.52
  428.2 2.9 fusion.54
  431.1 2.9 fusion.50
  434.0 2.7 fusion.48
  436.7 2.7 fusion.80
  439.4 2.7 fusion.14
  442.2 2.7 fusion.18
  444.9 9.6 %add_add_fusion.1 = f32[2,8,128,384]{2,3,1,0:T(8,128)} fusion(f32[2,8,128,384]{2,3,1,0:T(8,128)} %fusion.18, f32[2,8,128,384]{2,3,1,0:T(8,128)} %fusion.48, f32[2,8,128,384]{2,3,1,0:T(8,128)} %fusion.50, f32[2,8,128,384]{2,3,1,0:T(8,128)} %fusion.80, f32[2,8,128,384]{2,3,1,0:T(8,128)S(1)} %copy-done.10, f32[2,8,128,384]{2,3,1,0:T(8,128)} %fusion.54, ...), kind=kOutput, calls=%fused_computation.45 | convolution fusion | flops 510590976 | bytes 35520512 | tf_op jit(solution)/shard_map/bhwc,bcd->bhwd/dot_general | solution.py:46
  454.5 2.6 convert_reduce_fusion.1
  457.3 122.8 %psum.30 = f32[2,32]{1,0:T(2,128)S(1)} all-reduce(f32[2,32]{1,0:T(2,128)S(1)} %reduce_sum.82), channel_id=1, replica_groups=mesh['patch'=32,'req'=4,'owner'=2] {'patch','owner'}, use_global_device_ids=true, to_apply=%region_9.10 | all-reduce | flops 64 | bytes 512 | tf_op jit(solution)/shard_map/psum | solution.py:26
  581.0 127.5 %psum.31 = f32[2,32]{1,0:T(2,128)S(1)} all-reduce(f32[2,32]{1,0:T(2,128)S(1)} %reduce_sum.85), channel_id=1, replica_groups=mesh['patch'=32,'req'=4,'owner'=2] {'patch','owner'}, use_global_device_ids=true, to_apply=%region_12.13 | all-reduce | flops 64 | bytes 512 | tf_op jit(solution)/shard_map/psum | solution.py:29
  711.5 1.5 copy.166
  714.9 3.2 fusion.97
  718.1 1.8 collective-permute-done.5
  720.1 2.4 fusion.146
  722.5 1.9 copy.104
  725.7 1.9 copy.109
  727.7 3.7 collective-permute-start.7
  731.4 4.1 fusion.22
  735.5 2.7 fusion.26
  738.2 1.9 copy.105
  740.1 1.6 copy.110
  741.8 5.0 pad_maximum_fusion.1
  746.8 2.7 fusion.42
  749.5 2.7 fusion.38
  752.2 2.9 fusion.40
  755.1 2.9 fusion.36
  758.0 2.7 fusion.34
  760.7 8.9 %add_add_fusion = f32[2,8,128,384]{2,3,1,0:T(8,128)S(1)} fusion(f32[2,8,128,384]{2,3,1,0:T(8,128)} %fusion.26, f32[2,8,128,384]{2,3,1,0:T(8,128)} %fusion.34, f32[2,8,128,384]{2,3,1,0:T(8,128)} %fusion.36, f32[2,8,128,384]{2,3,1,0:T(8,128)S(1)} %copy-done.9, f32[2,8,128,384]{2,3,1,0:T(8,128)} %fusion.38, f32[2,8,128,384]{2,3,1,0:T(8,128)} %fusion.40, ...), kind=kOutput, calls=%fused_computation.44 | convolution fusion | flops 510590976 | bytes 35520512 | tf_op jit(solution)/shard_map/bhwc,bcd->bhwd/dot_general | solution.py:46
  769.6 1.6 fusion.11
  (100 shorter events, 17.5 us)
Async XLA Ops:
  6.5 375.3 %copy-start = (bf16[1280,320]{0,1:T(8,128)(2,1)S(1)}, bf16[1280,320]{0,1:T(8,128)(2,1)}, u32[]{:S(2)}) copy-start(bf16[1280,320]{0,1:T(8,128)(2,1)} %param.12) | copy-start | bytes 2457604
  6.5 184.9 %copy-start.5 = (bf16[2,8,128,320]{2,3,1,0:T(8,128)(2,1)S(1)}, bf16[2,8,128,320]{2,3,1,0:T(8,128)(2,1)}, u32[]{:S(2)}) copy-start(bf16[2,8,128,320]{2,3,1,0:T(8,128)(2,1)} %param.10) | copy-start | bytes 3932164
  6.5 309.9 %copy-start.15 = (f32[2,320]{1,0:T(2,128)S(1)}, f32[2,320]{1,0:T(2,128)}, u32[]{:S(2)}) copy-start(f32[2,320]{1,0:T(2,128)} %param.13) | copy-start | bytes 7684
  6.5 309.9 %copy-start.14 = (f32[2,320]{1,0:T(2,128)S(1)}, f32[2,320]{1,0:T(2,128)}, u32[]{:S(2)}) copy-start(f32[2,320]{1,0:T(2,128)} %param.14) | copy-start | bytes 7684
  6.5 397.2 %all-gather.2.cloned.1.call-start = ((), (), s32[]{:S(2)}) async-start(), calls=%async_computation | async-start | bytes 6635520 | tf_op jit(solution)/shard_map/all_gather | solution.py:78
  53.8 266.6 %copy-start.16 = (bf16[1,2,640]{2,1,0:T(2,128)(2,1)S(1)}, bf16[1,2,640]{2,1,0:T(2,128)(2,1)}, u32[]{:S(2)}) copy-start(bf16[1,2,640]{2,1,0:T(2,128)(2,1)} %param.17) | copy-start | bytes 7684
  317.9 64.4 %collective-permute-start = (bf16[2,1,128,320]{2,3,1,0:T(8,128)(2,1)S(1)}, bf16[2,1,128,320]{2,3,1,0:T(8,128)(2,1)S(1)}, u32[]{:S(2)}, u32[]{:S(2)}) collective-permute-start(bf16[2,1,128,320]{2,3,1,0:T(8,128)(2,1)S(1)} %get-tuple-element.23), channel_id=1, source_target_pairs={{0,8},{8,16},{16,24},{24,32},{32,40},{40,48},{48,56},{56,64},{64,7... | collective-permute-start | bytes 491528 | tf_op jit(solution)/shard_map/ppermute | solution.py:14
  319.2 63.1 %collective-permute-start.1 = (bf16[2,1,128,320]{2,3,1,0:T(8,128)(2,1)S(1)}, bf16[2,1,128,320]{2,3,1,0:T(8,128)(2,1)S(1)}, u32[]{:S(2)}, u32[]{:S(2)}) collective-permute-start(bf16[2,1,128,320]{2,3,1,0:T(8,128)(2,1)S(1)} %get-tuple-element.24), channel_id=1, source_target_pairs={{8,0},{16,8},{24,16},{32,24},{40,32},{48,40},{56,48},{64,56},{72,6... | collective-permute-start | bytes 491528 | tf_op jit(solution)/shard_map/ppermute | solution.py:17
  377.0 4.8 copy-start.13
  377.0 5.1 copy-start.17
  377.0 5.1 copy-start.18
  386.9 7.8 collective-permute-start.2
  390.1 6.3 collective-permute-start.3
  419.1 3.4 copy-start.12
  422.5 1.9 copy-start.8
  425.4 2.7 copy-start.7
  442.2 2.7 copy-start.10
  708.7 5.5 copy-start.11
  710.1 9.8 %copy-start.3 = (bf16[2,8,128,320]{2,3,1,0:T(8,128)(2,1)}, bf16[2,8,128,320]{2,3,1,0:T(8,128)(2,1)S(1)}, u32[]{:S(2)}) copy-start(bf16[2,8,128,320]{2,3,1,0:T(8,128)(2,1)S(1)} %multiply_convert_fusion) | copy-start | bytes 3932164
  710.2 7.9 %collective-permute-start.4 = (bf16[2,1,128,320]{2,3,1,0:T(8,128)(2,1)S(1)}, bf16[2,1,128,320]{2,3,1,0:T(8,128)(2,1)S(1)}, u32[]{:S(2)}, u32[]{:S(2)}) collective-permute-start(bf16[2,1,128,320]{2,3,1,0:T(8,128)(2,1)S(1)} %get-tuple-element.21), channel_id=1, source_target_pairs={{0,8},{8,16},{16,24},{24,32},{32,40},{40,48},{48,56},{56,64},{64,7... | collective-permute-start | bytes 491528 | tf_op jit(solution)/shard_map/ppermute | solution.py:14
  712.9 7.0 collective-permute-start.5
  714.8 3.2 copy-start.2
  724.4 13.8 %collective-permute-start.6 = (bf16[2,10,1,320]{3,0,2,1:T(2,128)(2,1)S(1)}, bf16[2,10,1,320]{3,0,2,1:T(2,128)(2,1)S(1)}, u32[]{:S(2)}, u32[]{:S(2)}) collective-permute-start(bf16[2,10,1,320]{3,0,2,1:T(2,128)(2,1)S(1)} %copy.104), channel_id=1, source_target_pairs={{0,1},{2,3},{4,5},{6,7},{8,9},{10,11},{12,13},{14,15},{16,17},{18,... | collective-permute-start | bytes 38408 | tf_op jit(solution)/shard_map/ppermute | solution.py:14
  725.7 9.8 %slice-start = ((s8[4423680]{0:T(1024)(128)(4,1)}), s8[229376]{0:T(1024)(128)(4,1)S(1)}, s32[]{:S(2)}) async-start(s8[4423680]{0:T(1024)(128)(4,1)} %bitcast.145), calls=%async_computation.1 | async-start | bytes 458752
  727.7 7.8 %slice-start.1 = ((s8[4423680]{0:T(1024)(128)(4,1)}), s8[4194304]{0:T(1024)(128)(4,1)S(1)}, s32[]{:S(2)}) async-start(s8[4423680]{0:T(1024)(128)(4,1)} %bitcast.145), calls=%async_computation.2 | async-start | bytes 8388608
  727.7 7.8 %copy-start.4 = (bf16[2,8,128,320]{2,3,1,0:T(8,128)(2,1)S(1)}, bf16[2,8,128,320]{2,3,1,0:T(8,128)(2,1)}, u32[]{:S(2)}) copy-start(bf16[2,8,128,320]{2,3,1,0:T(8,128)(2,1)} %copy-done.3) | copy-start | bytes 3932164
  727.7 12.5 %collective-permute-start.7 = (bf16[2,10,1,320]{3,0,2,1:T(2,128)(2,1)S(1)}, bf16[2,10,1,320]{3,0,2,1:T(2,128)(2,1)S(1)}, u32[]{:S(2)}, u32[]{:S(2)}) collective-permute-start(bf16[2,10,1,320]{3,0,2,1:T(2,128)(2,1)S(1)} %copy.109), channel_id=1, source_target_pairs={{1,0},{3,2},{5,4},{7,6},{9,8},{11,10},{13,12},{15,14},{17,16},{19,... | collective-permute-start | bytes 38408 | tf_op jit(solution)/shard_map/ppermute | solution.py:17
  740.1 6.7 slice-start.2
  741.8 5.0 slice-start.3
  758.0 2.7 copy-start.9
  760.7 8.9 %copy-start.6 = (bf16[2,8,128,320]{2,3,1,0:T(8,128)(2,1)S(1)}, bf16[2,8,128,320]{2,3,1,0:T(8,128)(2,1)}, u32[]{:S(2)}) copy-start(bf16[2,8,128,320]{2,3,1,0:T(8,128)(2,1)} %param.10) | copy-start | bytes 3932164
  760.7 10.6 %copy-start.1 = (bf16[1280,320]{0,1:T(8,128)(2,1)S(1)}, bf16[1280,320]{0,1:T(8,128)(2,1)}, u32[]{:S(2)}) copy-start(bf16[1280,320]{0,1:T(8,128)(2,1)} %param.12) | copy-start | bytes 2457604
Sparse Core Ops, SparseCore 0:
  54.0 51.1 all-gather.1
where the time goes:
time: 784 us; the launch traced here: 778 us
  blocking collectives  614 us (78%)
  matrix products  79 us (10%)
  local copies, waits for them, and re-layouts  37.7 us (5%)
  other arithmetic  17 us (2%)
  starting transfers between devices  15 us (2%)
  between operations  14.1 us (2%)
    psum x2, blocking collectives, group_act(): total = lax.psum(jnp.sum(grouped, axis=(1, 2, 4)), ('patch', 'owner'))  258 us
    psum x2, blocking collectives, group_act(): lax.psum(jnp.sum(centered * centered, axis=(1, 2, 4)), ('patch', 'owner'))  252 us
    dot_general x18, matrix products, block_conv(): jnp.einsum('bhwc,bcd->bhwd', window, joined[:, tap], preferred_element_ty...  62.9 us
    all_gather x1, blocking collectives, local(): lax.all_gather(plugin_reduce_library, 'patch', axis=2, tiled=True)  47.2 us
    all_gather x1, blocking collectives, local(): lax.all_gather(plugin_expand_library, 'patch', axis=2, tiled=True)  32 us
    all_gather x1, blocking collectives, local(): lax.all_gather(full_up, ('req', 'owner'), axis=0, tiled=True)  24.4 us
  transfers between devices with their start and end apart: 9, of which 1 were waited for; matrix products, arithmetic and copies ran while one was open for 5% of the time, Pallas kernels for 0%

commit v1 on v0

--- a/solution.py
+++ b/solution.py
@@ -26,7 +26,8 @@
     total = lax.psum(jnp.sum(grouped, axis=(1, 2, 4)), ("patch", "owner"))
     mean = total / count
     centered = grouped - mean[:, None, None, :, None]
-    spread = lax.psum(jnp.sum(centered * centered, axis=(1, 2, 4)), ("patch", "owner"))
+    partial = lax.psum(jnp.sum(centered * centered, axis=(1, 2, 4)), "owner")
+    spread = lax.psum(partial, "patch")
     var = spread / count
     normed = (centered / jnp.sqrt(var + 1e-05)[:, None, None, :, None]).reshape(values.shape)
     return jax.nn.silu(normed * gain + shift).astype(jnp.bfloat16)

time: 784 us -> 685 us (0.87)
  blocking collectives: 614 us -> 497 us
  starting transfers between devices: 15 us -> 33.1 us
    psum x2 -> x4, blocking collectives: 252 us -> 121 us  [the longest x2 112 us: group_act(): spread = lax.psum(partial, 'patch')]
    all_gather x1, blocking collectives: 24.4 us -> 38.2 us  [local(): lax.all_gather(full_up, ('req', 'owner'), axis=0, tiled=True)]
    ppermute x4, starting transfers between devices: 9.78 us -> 23.5 us  [padded_2(): lax.ppermute(lax.slice_in_dim(block, 0, width, axis=dim), axis, backward)]
  transfers between devices with their start and end apart: 9 -> 9, of which waited for: 1 -> 1; matrix products, arithmetic and copies ran while one was open for 5% -> 6% of each run, Pallas kernels for 0% -> 0%
where the time goes in v1:
time: 685 us; the launch traced here: 679 us
  blocking collectives  497 us (73%)
  matrix products  79 us (12%)
  local copies, waits for them, and re-layouts  37.7 us (6%)
  starting transfers between devices  33.1 us (5%)
  other arithmetic  17 us (2%)
  between operations  14.1 us (2%)
    psum x2, blocking collectives, group_act(): total = lax.psum(jnp.sum(grouped, axis=(1, 2, 4)), ('patch', 'owner'))  258 us
    psum x2, blocking collectives, group_act(): spread = lax.psum(partial, 'patch')  112 us
    dot_general x18, matrix products, block_conv(): jnp.einsum('bhwc,bcd->bhwd', window, joined[:, tap], preferred_element_ty...  62.9 us
    all_gather x1, blocking collectives, local(): lax.all_gather(plugin_reduce_library, 'patch', axis=2, tiled=True)  47.2 us
    all_gather x1, blocking collectives, local(): lax.all_gather(full_up, ('req', 'owner'), axis=0, tiled=True)  38.2 us
    all_gather x1, blocking collectives, local(): lax.all_gather(plugin_expand_library, 'patch', axis=2, tiled=True)  32 us
    ppermute x4, starting transfers between devices, padded_2(): lax.ppermute(lax.slice_in_dim(block, 0, width, axis=dim), axis, backward)  23.5 us
  transfers between devices with their start and end apart: 9, of which 1 were waited for; matrix products, arithmetic and copies ran while one was open for 6% of the time, Pallas kernels for 0%

profile of v1, /device:TPU:1, one launch (start us, length us, event | category | flops | bytes accessed | tf_op | source)
XLA Modules:
  0.0 679.0 jit_solution(7872060228628531882)
XLA Ops:
  6.6 47.2 %all_gather.12 = bf16[1,2,184320]{2,1,0:T(2,128)(2,1)} all-gather(bf16[1,2,5760]{2,1,0:T(2,128)(2,1)} %param.16), channel_id=1, replica_groups=mesh['patch'=32,'req'=4,'owner'=2] {'patch'}, dimensions={2}, use_global_device_ids=true | all-gather | bytes 760320 | tf_op jit(solution)/shard_map/all_gather | solution.py:75
  55.6 135.6 %psum.42 = f32[2,32]{1,0:T(2,128)S(1)} all-reduce(f32[2,32]{1,0:T(2,128)S(1)} %reduce_sum.59), channel_id=1, replica_groups=mesh['patch'=32,'req'=4,'owner'=2] {'patch','owner'}, use_global_device_ids=true, to_apply=%region_2.3 | all-reduce | flops 64 | bytes 512 | tf_op jit(solution)/shard_map/psum | solution.py:26
  192.2 2.8 psum.43
  194.9 56.0 %psum.44 = f32[2,32]{1,0:T(2,128)S(1)} all-reduce(f32[2,32]{1,0:T(2,128)S(1)} %psum.43), channel_id=1, replica_groups=mesh['patch'=32,'req'=4,'owner'=2] {'patch'}, use_global_device_ids=true, to_apply=%region_6.7 | all-reduce | flops 64 | bytes 512 | tf_op jit(solution)/shard_map/psum | solution.py:30
  252.6 3.5 collective-permute-start
  257.4 32.0 %all_gather.14 = bf16[1,2,20480]{2,1,0:T(2,128)(2,1)S(1)} all-gather(bf16[1,2,640]{2,1,0:T(2,128)(2,1)S(1)} %copy-done.16), channel_id=1, replica_groups=mesh['patch'=32,'req'=4,'owner'=2] {'patch'}, dimensions={2}, use_global_device_ids=true | all-gather | bytes 84480 | tf_op jit(solution)/shard_map/all_gather | solution.py:76
  289.4 38.2 %all_gather.15 = bf16[8,2,20480]{2,1,0:T(2,128)(2,1)S(1)} all-gather(bf16[1,2,20480]{2,1,0:T(2,128)(2,1)S(1)} %all_gather.14), channel_id=1, replica_groups=mesh['patch'=32,'req'=4,'owner'=2] {'req','owner'}, dimensions={0}, use_global_device_ids=true | all-gather | bytes 737280 | tf_op jit(solution)/shard_map/all_gather | solution.py:80
  327.6 4.8 slice_bitcast_fusion
  333.2 2.5 fusion.147
  335.7 1.9 copy.87
  338.8 1.9 copy.94
  340.7 3.5 collective-permute-start.3
  345.3 1.7 copy.88
  347.0 1.6 copy.95
  348.6 5.7 pad_maximum_fusion
  354.4 10.7 %convolution_convert_fusion = bf16[2,2,184320]{2,0,1:T(2,128)(2,1)} fusion(bf16[8,2,184320]{2,1,0:T(2,128)(2,1)} %all-gather.2.cloned.1.call-done, s32[2]{0:T(128)S(1)} %fusion.123), kind=kOutput, calls=%fused_computation | convolution fusion | flops 12533776 | bytes 7372808 | tf_op jit(solution)/shard_map/ik,kjs->ijs/dot_general | solution.py:84
  365.1 4.7 reshape.54
  369.7 3.3 fusion.145
  376.1 2.7 fusion.52
  378.8 2.9 fusion.54
  381.7 2.9 fusion.50
  384.6 2.7 fusion.48
  387.4 2.7 fusion.80
  390.1 2.7 fusion.14
  392.8 2.7 fusion.18
  395.5 9.6 %add_add_fusion.1 = f32[2,8,128,384]{2,3,1,0:T(8,128)} fusion(f32[2,8,128,384]{2,3,1,0:T(8,128)} %fusion.18, f32[2,8,128,384]{2,3,1,0:T(8,128)} %fusion.48, f32[2,8,128,384]{2,3,1,0:T(8,128)} %fusion.50, f32[2,8,128,384]{2,3,1,0:T(8,128)} %fusion.80, f32[2,8,128,384]{2,3,1,0:T(8,128)S(1)} %copy-done.10, f32[2,8,128,384]{2,3,1,0:T(8,128)} %fusion.54, ...), kind=kOutput, calls=%fused_computation.45 | convolution fusion | flops 510590976 | bytes 35520512 | tf_op jit(solution)/shard_map/bhwc,bcd->bhwd/dot_general | solution.py:47
  405.1 2.6 convert_reduce_fusion.1
  408.0 122.8 %psum.45 = f32[2,32]{1,0:T(2,128)S(1)} all-reduce(f32[2,32]{1,0:T(2,128)S(1)} %reduce_sum.82), channel_id=1, replica_groups=mesh['patch'=32,'req'=4,'owner'=2] {'patch','owner'}, use_global_device_ids=true, to_apply=%region_10.11 | all-reduce | flops 64 | bytes 512 | tf_op jit(solution)/shard_map/psum | solution.py:26
  531.7 6.0 psum.46
  537.7 56.2 %psum.47 = f32[2,32]{1,0:T(2,128)S(1)} all-reduce(f32[2,32]{1,0:T(2,128)S(1)} %psum.46), channel_id=1, replica_groups=mesh['patch'=32,'req'=4,'owner'=2] {'patch'}, use_global_device_ids=true, to_apply=%region_14.15 | all-reduce | flops 64 | bytes 512 | tf_op jit(solution)/shard_map/psum | solution.py:30
  595.5 3.5 collective-permute-start.4
  602.4 3.2 fusion.97
  607.0 2.4 fusion.146
  609.4 1.9 copy.104
  612.6 1.9 copy.109
  614.6 17.4 %collective-permute-start.7 = (bf16[2,10,1,320]{3,0,2,1:T(2,128)(2,1)S(1)}, bf16[2,10,1,320]{3,0,2,1:T(2,128)(2,1)S(1)}, u32[]{:S(2)}, u32[]{:S(2)}) collective-permute-start(bf16[2,10,1,320]{3,0,2,1:T(2,128)(2,1)S(1)} %copy.109), channel_id=1, source_target_pairs={{1,0},{3,2},{5,4},{7,6},{9,8},{11,10},{13,12},{15,14},{17,16},{19,... | collective-permute-start | bytes 38408 | tf_op jit(solution)/shard_map/ppermute | solution.py:17
  632.0 4.1 fusion.22
  636.1 2.7 fusion.26
  638.8 1.9 copy.105
  640.7 1.6 copy.110
  642.4 5.0 pad_maximum_fusion.1
  647.4 2.7 fusion.42
  650.1 2.7 fusion.38
  652.8 2.9 fusion.40
  655.7 2.9 fusion.36
  658.6 2.7 fusion.34
  661.3 8.9 %add_add_fusion = f32[2,8,128,384]{2,3,1,0:T(8,128)S(1)} fusion(f32[2,8,128,384]{2,3,1,0:T(8,128)} %fusion.26, f32[2,8,128,384]{2,3,1,0:T(8,128)} %fusion.34, f32[2,8,128,384]{2,3,1,0:T(8,128)} %fusion.36, f32[2,8,128,384]{2,3,1,0:T(8,128)S(1)} %copy-done.9, f32[2,8,128,384]{2,3,1,0:T(8,128)} %fusion.38, f32[2,8,128,384]{2,3,1,0:T(8,128)} %fusion.40, ...), kind=kOutput, calls=%fused_computation.44 | convolution fusion | flops 510590976 | bytes 35520512 | tf_op jit(solution)/shard_map/bhwc,bcd->bhwd/dot_general | solution.py:47
  670.2 1.6 fusion.11
  (102 shorter events, 20.5 us)
Async XLA Ops:
  6.5 325.9 %copy-start = (bf16[1280,320]{0,1:T(8,128)(2,1)S(1)}, bf16[1280,320]{0,1:T(8,128)(2,1)}, u32[]{:S(2)}) copy-start(bf16[1280,320]{0,1:T(8,128)(2,1)} %param.12) | copy-start | bytes 2457604
  6.5 184.9 %copy-start.5 = (bf16[2,8,128,320]{2,3,1,0:T(8,128)(2,1)S(1)}, bf16[2,8,128,320]{2,3,1,0:T(8,128)(2,1)}, u32[]{:S(2)}) copy-start(bf16[2,8,128,320]{2,3,1,0:T(8,128)(2,1)} %param.10) | copy-start | bytes 3932164
  6.5 244.6 %copy-start.15 = (f32[2,320]{1,0:T(2,128)S(1)}, f32[2,320]{1,0:T(2,128)}, u32[]{:S(2)}) copy-start(f32[2,320]{1,0:T(2,128)} %param.13) | copy-start | bytes 7684
  6.5 244.6 %copy-start.14 = (f32[2,320]{1,0:T(2,128)S(1)}, f32[2,320]{1,0:T(2,128)}, u32[]{:S(2)}) copy-start(f32[2,320]{1,0:T(2,128)} %param.14) | copy-start | bytes 7684
  6.5 347.8 %all-gather.2.cloned.1.call-start = ((), (), s32[]{:S(2)}) async-start(), calls=%async_computation | async-start | bytes 6635520 | tf_op jit(solution)/shard_map/all_gather | solution.py:79
  53.8 203.5 %copy-start.16 = (bf16[1,2,640]{2,1,0:T(2,128)(2,1)S(1)}, bf16[1,2,640]{2,1,0:T(2,128)(2,1)}, u32[]{:S(2)}) copy-start(bf16[1,2,640]{2,1,0:T(2,128)(2,1)} %param.17) | copy-start | bytes 7684
  252.6 80.4 %collective-permute-start = (bf16[2,1,128,320]{2,3,1,0:T(8,128)(2,1)S(1)}, bf16[2,1,128,320]{2,3,1,0:T(8,128)(2,1)S(1)}, u32[]{:S(2)}, u32[]{:S(2)}) collective-permute-start(bf16[2,1,128,320]{2,3,1,0:T(8,128)(2,1)S(1)} %get-tuple-element.23), channel_id=1, source_target_pairs={{0,8},{8,16},{16,24},{24,32},{32,40},{40,48},{48,56},{56,64},{64,7... | collective-permute-start | bytes 491528 | tf_op jit(solution)/shard_map/ppermute | solution.py:14
  256.1 76.9 %collective-permute-start.1 = (bf16[2,1,128,320]{2,3,1,0:T(8,128)(2,1)S(1)}, bf16[2,1,128,320]{2,3,1,0:T(8,128)(2,1)S(1)}, u32[]{:S(2)}, u32[]{:S(2)}) collective-permute-start(bf16[2,1,128,320]{2,3,1,0:T(8,128)(2,1)S(1)} %get-tuple-element.24), channel_id=1, source_target_pairs={{8,0},{16,8},{24,16},{32,24},{40,32},{48,40},{56,48},{64,56},{72,6... | collective-permute-start | bytes 491528 | tf_op jit(solution)/shard_map/ppermute | solution.py:17
  327.6 4.8 copy-start.13
  327.6 5.1 copy-start.17
  327.6 5.1 copy-start.18
  337.5 7.8 %collective-permute-start.2 = (bf16[2,10,1,320]{3,0,2,1:T(2,128)(2,1)S(1)}, bf16[2,10,1,320]{3,0,2,1:T(2,128)(2,1)S(1)}, u32[]{:S(2)}, u32[]{:S(2)}) collective-permute-start(bf16[2,10,1,320]{3,0,2,1:T(2,128)(2,1)S(1)} %copy.87), channel_id=1, source_target_pairs={{0,1},{2,3},{4,5},{6,7},{8,9},{10,11},{12,13},{14,15},{16,17},{18,... | collective-permute-start | bytes 38408 | tf_op jit(solution)/shard_map/ppermute | solution.py:14
  340.7 6.3 collective-permute-start.3
  369.7 3.4 copy-start.12
  373.1 1.9 copy-start.8
  376.1 2.7 copy-start.7
  392.8 2.7 copy-start.10
  594.0 7.7 %copy-start.11 = (bf16[9,320,320]{2,1,0:T(8,128)(2,1)S(1)}, bf16[9,320,320]{2,1,0:T(8,128)(2,1)}, u32[]{:S(2)}) copy-start(bf16[9,320,320]{2,1,0:T(8,128)(2,1)} %get-tuple-element.9) | copy-start | bytes 5529604
  595.4 11.4 %copy-start.3 = (bf16[2,8,128,320]{2,3,1,0:T(8,128)(2,1)}, bf16[2,8,128,320]{2,3,1,0:T(8,128)(2,1)S(1)}, u32[]{:S(2)}) copy-start(bf16[2,8,128,320]{2,3,1,0:T(8,128)(2,1)S(1)} %multiply_convert_fusion) | copy-start | bytes 3932164
  595.5 10.1 %collective-permute-start.4 = (bf16[2,1,128,320]{2,3,1,0:T(8,128)(2,1)S(1)}, bf16[2,1,128,320]{2,3,1,0:T(8,128)(2,1)S(1)}, u32[]{:S(2)}, u32[]{:S(2)}) collective-permute-start(bf16[2,1,128,320]{2,3,1,0:T(8,128)(2,1)S(1)} %get-tuple-element.21), channel_id=1, source_target_pairs={{0,8},{8,16},{16,24},{24,32},{32,40},{40,48},{48,56},{56,64},{64,7... | collective-permute-start | bytes 491528 | tf_op jit(solution)/shard_map/ppermute | solution.py:14
  600.4 6.4 collective-permute-start.5
  602.3 3.2 copy-start.2
  611.3 27.6 %collective-permute-start.6 = (bf16[2,10,1,320]{3,0,2,1:T(2,128)(2,1)S(1)}, bf16[2,10,1,320]{3,0,2,1:T(2,128)(2,1)S(1)}, u32[]{:S(2)}, u32[]{:S(2)}) collective-permute-start(bf16[2,10,1,320]{3,0,2,1:T(2,128)(2,1)S(1)} %copy.104), channel_id=1, source_target_pairs={{0,1},{2,3},{4,5},{6,7},{8,9},{10,11},{12,13},{14,15},{16,17},{18,... | collective-permute-start | bytes 38408 | tf_op jit(solution)/shard_map/ppermute | solution.py:14
  612.6 23.5 %slice-start = ((s8[4423680]{0:T(1024)(128)(4,1)}), s8[229376]{0:T(1024)(128)(4,1)S(1)}, s32[]{:S(2)}) async-start(s8[4423680]{0:T(1024)(128)(4,1)} %bitcast.145), calls=%async_computation.1 | async-start | bytes 458752
  614.5 21.6 %slice-start.1 = ((s8[4423680]{0:T(1024)(128)(4,1)}), s8[4194304]{0:T(1024)(128)(4,1)S(1)}, s32[]{:S(2)}) async-start(s8[4423680]{0:T(1024)(128)(4,1)} %bitcast.145), calls=%async_computation.2 | async-start | bytes 8388608
  614.5 21.6 %copy-start.4 = (bf16[2,8,128,320]{2,3,1,0:T(8,128)(2,1)S(1)}, bf16[2,8,128,320]{2,3,1,0:T(8,128)(2,1)}, u32[]{:S(2)}) copy-start(bf16[2,8,128,320]{2,3,1,0:T(8,128)(2,1)} %copy-done.3) | copy-start | bytes 3932164
  614.6 26.2 %collective-permute-start.7 = (bf16[2,10,1,320]{3,0,2,1:T(2,128)(2,1)S(1)}, bf16[2,10,1,320]{3,0,2,1:T(2,128)(2,1)S(1)}, u32[]{:S(2)}, u32[]{:S(2)}) collective-permute-start(bf16[2,10,1,320]{3,0,2,1:T(2,128)(2,1)S(1)} %copy.109), channel_id=1, source_target_pairs={{1,0},{3,2},{5,4},{7,6},{9,8},{11,10},{13,12},{15,14},{17,16},{19,... | collective-permute-start | bytes 38408 | tf_op jit(solution)/shard_map/ppermute | solution.py:17
  640.7 6.7 slice-start.2
  642.4 5.0 slice-start.3
  658.6 2.7 copy-start.9
  661.3 8.9 %copy-start.6 = (bf16[2,8,128,320]{2,3,1,0:T(8,128)(2,1)S(1)}, bf16[2,8,128,320]{2,3,1,0:T(8,128)(2,1)}, u32[]{:S(2)}) copy-start(bf16[2,8,128,320]{2,3,1,0:T(8,128)(2,1)} %param.10) | copy-start | bytes 3932164
  661.3 10.6 %copy-start.1 = (bf16[1280,320]{0,1:T(8,128)(2,1)S(1)}, bf16[1280,320]{0,1:T(8,128)(2,1)}, u32[]{:S(2)}) copy-start(bf16[1280,320]{0,1:T(8,128)(2,1)} %param.12) | copy-start | bytes 2457604
Sparse Core Ops, SparseCore 0:
  54.0 51.1 all-gather.1
